TPU v7x, 512 devices: a whole 4x4x16 slice. The times are simulated.
512 devices in a mesh: dp: 8 (over y_hi, x), tile: 64 (over y_lo, z, core).
Axes of the slice: x: 4, y: 4 (y_hi: 2, y_lo: 2; y = y_hi * 2 + y_lo), z: 16, core: 2. Of those that a mesh axis runs over, the one named last changes fastest.
Arguments:
- ocean_state: bfloat16 [8, 256, 64, 768], P('dp', 'tile'), may hold values from -6 to 6
- cotangent: bfloat16 [8, 256, 64, 768], P('dp', 'tile'), may hold values from -6 to 6
- depth_kernel: float32 [7, 7, 768], replicated, may hold values from -0.875 to 0.875
- norm_gain: float32 [768], replicated, may hold values from 0.5 to 2
- expand_weight: bfloat16 [768, 3072], P('tile'), may hold values from -0.21875 to 0.21875
- expand_bias: float32 [3072], replicated, may hold values from -4 to 4
- reduce_weight: bfloat16 [3072, 768], P('tile'), may hold values from -0.109375 to 0.109375
- tile_slot: int32 [256], P('tile'), may hold values from -1 to 5, as said below
Outputs:
- state_grad: bfloat16 [8, 256, 64, 768], P('dp', 'tile')
- kernel_grad: float32 [7, 7, 768], replicated
- gain_grad: float32 [768], replicated
- bias_grad: float32 [3072], replicated
Inputs may be any that keep to these rules, and one draw needn't show every extreme that they name: `tile_slot`: entry t is -1 for a land tile, k < 3 for slot k of the tile's own device, 3 + k for slot k of the device whose tile index differs by half of the axis; the tiles of a device and of that device together name each slot of either at most once, and on some pair of devices every slot is named.
All inputs are finite; a program needn't handle non-finite values.
Results may differ from a plain program's by a relative error of at most 0.0085.
Values may be sent and summed in bfloat16 or wider, within the bound.
No kernel may reach another device: no remote copies, remote signals or barrier semaphores. Data moves between devices by JAX's collectives and lax.ppermute only.
A program may use at most 64 MiB of HBM per device.

v0:
```python
import math
import jax
import jax.numpy as jnp
from jax import lax
from jax.sharding import PartitionSpec as P

KS = 7


def with_halo(cells, sides, width):
    for axis, dim in sides:
        count = lax.axis_size(axis)
        ends = count - 1
        head = lax.slice_in_dim(cells, 0, width, axis=dim)
        tail = lax.slice_in_dim(cells, cells.shape[dim] - width, cells.shape[dim], axis=dim)
        cells = jnp.concatenate(
            [
                lax.ppermute(tail, axis, [(i, (i + 1) % count) for i in range(ends)]),
                cells,
                lax.ppermute(head, axis, [((i + 1) % count, i) for i in range(ends)]),
            ],
            axis=dim,
        )
    return cells


def depthwise(padded, kernel, row_count, col_count):
    total = None
    for shift_row in range(KS):
        band = padded[..., shift_row : shift_row + row_count, :, :]
        part = kernel[shift_row, 0] * band[..., 0:col_count, :].astype(jnp.float32)
        for shift_col in range(1, KS):
            part = part + kernel[shift_row, shift_col] * band[
                ..., shift_col : shift_col + col_count, :
            ].astype(jnp.float32)
        total = part if total is None else total + part
    return total


def gelu_slope(value):
    factor = math.sqrt(2.0 / math.pi)
    inner = factor * (value + 0.044715 * value * value * value)
    tangent = jnp.tanh(inner)
    return 0.5 * (1.0 + tangent) + 0.5 * value * (1.0 - tangent * tangent) * factor * (
        1.0 + 3.0 * 0.044715 * value * value
    )


def local(
    ocean_state,
    cotangent,
    depth_kernel,
    norm_gain,
    expand_weight,
    expand_bias,
    reduce_weight,
    tile_slot,
):
    samples, row_count, col_count, channels = ocean_state.shape
    tile_count = tile_slot.shape[0]
    tile_rows = row_count // tile_count
    rim = KS // 2
    padded = with_halo(ocean_state, (("tile", 1),), rim)
    padded = jnp.pad(padded, ((0, 0), (0, 0), (rim, rim), (0, 0)))
    mixed = depthwise(padded, depth_kernel, row_count, col_count)
    centred = mixed - jnp.mean(mixed, axis=-1, keepdims=True)
    inverse = lax.rsqrt(jnp.mean(centred * centred, axis=-1, keepdims=True) + 1e-06)
    normed = centred * inverse
    scaled = (normed * norm_gain).astype(jnp.bfloat16)
    row_mask = jnp.repeat(tile_slot >= 0, tile_rows).astype(jnp.bfloat16)
    masked = cotangent * row_mask[None, :, None, None]
    contract_last = (((1,), (1,)), ((), ()))
    full_expand, full_reduce = (
        lax.all_gather(expand_weight, "tile", axis=0, tiled=True),
        lax.all_gather(reduce_weight, "tile", axis=0, tiled=True),
    )
    hidden = (
        jnp.dot(scaled.reshape(-1, channels), full_expand, preferred_element_type=jnp.float32)
        + expand_bias
    )
    back_act = lax.dot_general(
        masked.reshape(-1, channels), full_reduce, contract_last, preferred_element_type=jnp.float32
    )
    back_hidden = (back_act * gelu_slope(hidden)).astype(jnp.bfloat16)
    back_scaled = lax.dot_general(
        back_hidden, full_expand, contract_last, preferred_element_type=jnp.float32
    ).astype(jnp.bfloat16)
    scaled_back = back_scaled
    bias_part = jnp.sum(back_hidden.astype(jnp.float32), axis=0)
    back_scaled = scaled_back.reshape(samples, row_count, col_count, channels)
    back_float = back_scaled.astype(jnp.float32)
    gain_part = jnp.sum(back_float * normed, axis=(0, 1, 2))
    back_norm = back_float * norm_gain
    back_mixed = inverse * (
        back_norm
        - jnp.mean(back_norm, axis=-1, keepdims=True)
        - normed * jnp.mean(back_norm * normed, axis=-1, keepdims=True)
    )
    back_mixed = back_mixed.astype(jnp.bfloat16)
    mixed_float = back_mixed.astype(jnp.float32)
    kernel_rows = []
    for shift_row in range(KS):
        band = padded[:, shift_row : shift_row + row_count, :, :]
        kernel_cols = [
            jnp.sum(
                band[:, :, shift_col : shift_col + col_count, :].astype(jnp.float32) * mixed_float,
                axis=(0, 1, 2),
            )
            for shift_col in range(KS)
        ]
        kernel_rows.append(jnp.stack(kernel_cols))
    kernel_part = jnp.stack(kernel_rows)
    back_padded = with_halo(back_mixed, (("tile", 1),), rim)
    back_padded = jnp.pad(back_padded, ((0, 0), (0, 0), (rim, rim), (0, 0)))
    through = depthwise(back_padded, depth_kernel[::-1, ::-1], row_count, col_count)
    state_grad = (cotangent.astype(jnp.float32) + through).astype(jnp.bfloat16)
    kernel_grad, gain_grad, bias_grad = lax.psum(
        (kernel_part, gain_part, bias_part), ("dp", "tile")
    )
    return (state_grad, kernel_grad, gain_grad, bias_grad)


def solution(mesh):
    return jax.shard_map(
        local,
        mesh=mesh,
        in_specs=(
            P("dp", "tile", None, None),
            P("dp", "tile", None, None),
            P(),
            P(),
            P("tile", None),
            P(),
            P("tile", None),
            P("tile"),
        ),
        out_specs=(P("dp", "tile", None, None), P(), P(), P()),
        check_vma=False,
    )
```

profile of v0, /device:TPU:1, one launch (start us, length us, event | category | flops | bytes accessed | tf_op | source)
XLA Modules:
  0.0 757.2 jit_solution(15072238544217701571)
XLA Ops:
  7.2 0.7 all-gather.6.cloned.1.call-update
  8.0 0.7 all-gather.4.cloned.1.call-update
  8.7 1.1 fusion.127
  9.8 4.9 collective-permute-start
  14.7 5.1 collective-permute-start.1
  19.9 0.7 compare_convert_fusion
  20.5 1.9 broadcast_multiply_fusion
  22.4 1.4 slice_reduce_fusion.48
  23.8 0.2 slice_reduce_fusion.47
  24.3 0.3 fusion.12
  24.7 6.4 fusion.124
  31.1 0.2 multiply_reduce_fusion.3
  31.4 0.9 multiply_convert_fusion.1
  32.3 109.8 %all-gather.6.cloned.1.call-done = bf16[64,12,3072]{2,1,0:T(8,128)(2,1)} async-done(((bf16[1,12,3072]{2,1,0:T(8,128)(2,1)}), bf16[64,12,3072]{2,1,0:T(8,128)(2,1)}) %all-gather.6.cloned.1.call-update) | async-done | bytes 4718608 | tf_op jit(solution)/shard_map/all_gather | solution.py:74
  142.1 7.5 reshape.394
  149.6 5.5 convolution_add_fusion
  155.2 109.3 %all-gather.4.cloned.1.call-done = bf16[3072,768]{1,0:T(8,128)(2,1)} async-done(((bf16[48,768]{1,0:T(8,128)(2,1)}), bf16[3072,768]{1,0:T(8,128)(2,1)}) %all-gather.4.cloned.1.call-update) | async-done | bytes 4718608 | tf_op jit(solution)/shard_map/all_gather | solution.py:75
  264.5 7.3 convert_reduce_fusion
  271.8 2.3 multiply_reduce_fusion.2
  274.1 0.7 div.17
  274.7 2.4 multiply_reduce_fusion
  277.1 3.7 fusion.118
  280.9 1.2 fusion.117
  282.1 2.0 fusion.119
  284.8 3.3 collective-permute-start.2
  288.1 2.1 collective-permute-start.3
  290.7 0.7 copy-done.7
  291.4 102.4 %all-reduce.2 = (f32[768]{0:T(1024)}, f32[3072]{0:T(1024)}) all-reduce(f32[768]{0:T(1024)S(1)} %copy-done.24, f32[3072]{0:T(1024)S(1)} %copy-done.25), channel_id=1, replica_groups=mesh['dp'=8,'tile'=64] {'dp','tile'}, use_global_device_ids=true, to_apply=%region_55.56 | all-reduce | flops 3840 | bytes 30720 | tf_op jit(solution)/shard_map/psum | solution.py:117
  393.8 0.3 select_maximum_fusion
  394.2 6.5 fusion.70
  400.7 348.3 %all-reduce.5.cloned.1.call-done = f32[7,7,768]{2,1,0:T(8,128)} async-done(((f32[7,7,768]{2,1,0:T(8,128)}), f32[7,7,768]{2,1,0:T(8,128)}) %all-reduce.5.cloned.1.call-update) | async-done | bytes 150544 | tf_op jit(solution)/shard_map/psum | solution.py:117
  749.0 1.6 copy.21
  (133 shorter events, 1.2 us)
Async XLA Ops:
  7.2 17.0 %copy-start = (bf16[1,4,64,768]{3,2,1,0:T(8,128)(2,1)S(1)}, bf16[1,4,64,768]{3,2,1,0:T(8,128)(2,1)}, u32[]{:S(2)}) copy-start(bf16[1,4,64,768]{3,2,1,0:T(8,128)(2,1)} %param.8) | copy-start | bytes 1179652
  7.2 16.6 %copy-start.8 = (f32[7,7,768]{2,1,0:T(8,128)S(1)}, f32[7,7,768]{2,1,0:T(8,128)}, u32[]{:S(2)}) copy-start(f32[7,7,768]{2,1,0:T(8,128)} %param.10) | copy-start | bytes 451588
  7.2 134.9 %all-gather.6.cloned.1.call-start = ((), (), s32[]{:S(2)}) async-start(), calls=%async_computation.2 | async-start | bytes 6389760 | tf_op jit(solution)/shard_map/all_gather | solution.py:74
  7.9 256.6 %all-gather.4.cloned.1.call-start = ((), (), s32[]{:S(2)}) async-start(), calls=%async_computation | async-start | bytes 4792320 | tf_op jit(solution)/shard_map/all_gather | solution.py:75
  8.7 740.4 %all-reduce.5.cloned.1.call-start = ((), (), s32[]{:S(2)}) async-start(), calls=%async_computation.1 | async-start | bytes 344064 | tf_op jit(solution)/shard_map/psum | solution.py:117
  9.8 14.3 %collective-permute-start = (bf16[1,3,64,768]{3,2,1,0:T(8,128)(2,1)S(1)}, bf16[1,3,64,768]{3,2,1,0:T(8,128)(2,1)S(1)}, u32[]{:S(2)}, u32[]{:S(2)}) collective-permute-start(bf16[1,3,64,768]{3,2,1,0:T(8,128)(2,1)S(1)} %get-tuple-element.119), channel_id=1, source_target_pairs={{0,1},{1,2},{2,3},{3,4},{4,5},{5,6},{6,7},{7,8},{8,9},{9,10},{10,1... | collective-permute-start | bytes 884744 | tf_op jit(solution)/shard_map/ppermute | solution.py:18
  14.7 9.5 %collective-permute-start.1 = (bf16[1,3,64,768]{3,2,1,0:T(8,128)(2,1)S(1)}, bf16[1,3,64,768]{3,2,1,0:T(8,128)(2,1)S(1)}, u32[]{:S(2)}, u32[]{:S(2)}) collective-permute-start(bf16[1,3,64,768]{3,2,1,0:T(8,128)(2,1)S(1)} %get-tuple-element.120), channel_id=1, source_target_pairs={{1,0},{2,1},{3,2},{4,3},{5,4},{6,5},{7,6},{8,7},{9,8},{10,9},{11,1... | collective-permute-start | bytes 884744 | tf_op jit(solution)/shard_map/ppermute | solution.py:20
  24.1 0.6 copy-start.10
  24.1 0.6 copy-start.14
  24.1 0.6 copy-start.18
  24.2 6.9 copy-start.1
  24.7 6.7 copy-start.9
  31.4 118.3 %copy-start.20 = (f32[4,64]{1,0:T(4,128)}, f32[4,64]{1,0:T(4,128)S(1)}, u32[]{:S(2)}) copy-start(f32[4,64]{1,0:T(4,128)S(1)} %add_rsqrt_fusion) | copy-start | bytes 3076
  149.6 114.8 %copy-start.6 = (bf16[1,4,64,768]{3,2,1,0:T(8,128)(2,1)S(1)}, bf16[1,4,64,768]{3,2,1,0:T(8,128)(2,1)}, u32[]{:S(2)}) copy-start(bf16[1,4,64,768]{3,2,1,0:T(8,128)(2,1)} %broadcast_multiply_fusion) | copy-start | bytes 1179652
  264.5 7.3 copy-start.4
  271.8 3.0 copy-start.21
  274.7 2.4 copy-start.3
  274.7 2.4 copy-start.26
  277.1 3.7 copy-start.2
  282.0 8.5 %copy-start.23 = (f32[768]{0:T(1024)S(1)}, f32[768]{0:T(1024)}, u32[]{:S(2)}) copy-start(f32[768]{0:T(1024)} %get-tuple-element.22) | copy-start | bytes 9220
  282.0 8.5 %copy-start.22 = (f32[768]{0:T(1024)S(1)}, f32[768]{0:T(1024)}, u32[]{:S(2)}) copy-start(f32[768]{0:T(1024)} %get-tuple-element.39) | copy-start | bytes 9220
  284.1 7.3 copy-start.24
  284.1 7.3 copy-start.25
  284.1 110.1 %copy-start.5 = (bf16[1,4,64,768]{3,2,1,0:T(8,128)(2,1)S(1)}, bf16[1,4,64,768]{3,2,1,0:T(8,128)(2,1)}, u32[]{:S(2)}) copy-start(bf16[1,4,64,768]{3,2,1,0:T(8,128)(2,1)} %param.9) | copy-start | bytes 1179652
  284.1 110.1 %copy-start.11 = (f32[768]{0:T(1024)S(1)}, f32[768]{0:T(1024)}, u32[]{:S(2)}) copy-start(f32[768]{0:T(1024)} %copy-done.10) | copy-start | bytes 9220
  284.1 110.1 %copy-start.13 = (f32[768]{0:T(1024)S(1)}, f32[768]{0:T(1024)}, u32[]{:S(2)}) copy-start(f32[768]{0:T(1024)} %copy-done.12) | copy-start | bytes 9220
  284.1 110.1 %copy-start.15 = (f32[768]{0:T(1024)S(1)}, f32[768]{0:T(1024)}, u32[]{:S(2)}) copy-start(f32[768]{0:T(1024)} %copy-done.14) | copy-start | bytes 9220
  284.1 110.1 %copy-start.17 = (f32[768]{0:T(1024)S(1)}, f32[768]{0:T(1024)}, u32[]{:S(2)}) copy-start(f32[768]{0:T(1024)} %copy-done.16) | copy-start | bytes 9220
  284.1 110.1 %copy-start.19 = (f32[768]{0:T(1024)S(1)}, f32[768]{0:T(1024)}, u32[]{:S(2)}) copy-start(f32[768]{0:T(1024)} %copy-done.18) | copy-start | bytes 9220
  284.8 109.1 %collective-permute-start.2 = (bf16[1,3,64,768]{3,2,1,0:T(8,128)(2,1)S(1)}, bf16[1,3,64,768]{3,2,1,0:T(8,128)(2,1)S(1)}, u32[]{:S(2)}, u32[]{:S(2)}) collective-permute-start(bf16[1,3,64,768]{3,2,1,0:T(8,128)(2,1)S(1)} %get-tuple-element.115), channel_id=1, source_target_pairs={{0,1},{1,2},{2,3},{3,4},{4,5},{5,6},{6,7},{7,8},{8,9},{9,10},{10,1... | collective-permute-start | bytes 884744 | tf_op jit(solution)/shard_map/ppermute | solution.py:18
  288.1 105.7 %collective-permute-start.3 = (bf16[1,3,64,768]{3,2,1,0:T(8,128)(2,1)S(1)}, bf16[1,3,64,768]{3,2,1,0:T(8,128)(2,1)S(1)}, u32[]{:S(2)}, u32[]{:S(2)}) collective-permute-start(bf16[1,3,64,768]{3,2,1,0:T(8,128)(2,1)S(1)} %get-tuple-element.116), channel_id=1, source_target_pairs={{1,0},{2,1},{3,2},{4,3},{5,4},{6,5},{7,6},{8,7},{9,8},{10,9},{11,1... | collective-permute-start | bytes 884744 | tf_op jit(solution)/shard_map/ppermute | solution.py:20
  290.7 0.7 copy-start.7
  (2 other events, 1.2 us)
Sparse Core Ops, SparseCore 0:
  10.1 131.8 all-gather.5
  144.2 120.1 all-gather.3
  291.5 457.4 all-reduce.4
where the time goes:
time: 758 us; the launch traced here: 757 us
  waiting for transfers between devices  569 us (75%)
  blocking collectives  102 us (13%)
  other arithmetic  26.5 us (3%)
  starting transfers between devices  15.6 us (2%)
  matrix products  15.1 us (2%)
  between operations  14.6 us (2%)
  local copies, waits for them, and re-layouts  14.1 us (2%)
    psum x1, waiting for transfers between devices, local(): lax.psum((kernel_part, gain_part, bias_part), ('dp', 'tile'))  348 us
    all_gather x1, waiting for transfers between devices, local(): lax.all_gather(expand_weight, 'tile', axis=0, tiled=True)  110 us
    all_gather x1, waiting for transfers between devices, local(): lax.all_gather(reduce_weight, 'tile', axis=0, tiled=True)  109 us
    psum x1, blocking collectives, local(): lax.psum((kernel_part, gain_part, bias_part), ('dp', 'tile'))  102 us
  transfers between devices with their start and end apart: 7, of which 3 were waited for; matrix products, arithmetic and copies ran while one was open for 4% of the time, Pallas kernels for 0%

commit v1 on v0

--- a/solution.py
+++ b/solution.py
@@ -1,3 +1,4 @@
+import functools
 import math
 import jax
 import jax.numpy as jnp
@@ -5,6 +6,16 @@
 from jax.sharding import PartitionSpec as P
 
 KS = 7
+
+
+def bring_signs_by_axis(in_array, group_axis):
+    next_value = jax.lax.all_to_all(
+        jnp.stack(jax.lax.axis_size(group_axis) * [in_array]), group_axis, 0, 0
+    )
+    return jnp.concatenate(next_value, 0)
+
+
+rings_show = functools.partial(bring_signs_by_axis, group_axis="tile")
 
 
 def with_halo(cells, sides, width):
@@ -72,7 +83,7 @@
     contract_last = (((1,), (1,)), ((), ()))
     full_expand, full_reduce = (
         lax.all_gather(expand_weight, "tile", axis=0, tiled=True),
-        lax.all_gather(reduce_weight, "tile", axis=0, tiled=True),
+        rings_show(reduce_weight),
     )
     hidden = (
         jnp.dot(scaled.reshape(-1, channels), full_expand, preferred_element_type=jnp.float32)

time: 758 us -> 787 us (1.038)
  starting transfers between devices: 15.6 us -> 28.5 us
  waiting for transfers between devices: 569 us -> 581 us
    ppermute x2, waiting for transfers between devices: 0.01 us -> 229 us  [with_halo(): lax.ppermute(tail, axis, [(i, (i + 1) % count) for i in range(ends)])]
    all_gather x1, waiting for transfers between devices: 110 us -> 0.19 us  [local(): lax.all_gather(expand_weight, 'tile', axis=0, tiled=True)]
    all_gather x1 -> x0, waiting for transfers between devices: 109 us -> none  [local(): lax.all_gather(reduce_weight, 'tile', axis=0, tiled=True)]
    all_to_all x0 -> x1, starting transfers between devices: none -> 18.5 us  [bring_signs_by_axis(): jax.lax.all_to_all(jnp.stack(jax.lax.axis_size(group_axis) * [in_array]),...]
  transfers between devices with their start and end apart: 7 -> 7, of which waited for: 3 -> 4; matrix products, arithmetic and copies ran while one was open for 4% -> 4% of each run, Pallas kernels for 0% -> 0%
where the time goes in v1:
time: 787 us
  waiting for transfers between devices  581 us (74%)
  blocking collectives  108 us (14%)
  starting transfers between devices  28.5 us (4%)
  other arithmetic  24.2 us (3%)
  local copies, waits for them, and re-layouts  16 us (2%)
  between operations  14.9 us (2%)
  matrix products  14.3 us (2%)
    psum x1, waiting for transfers between devices, local(): lax.psum((kernel_part, gain_part, bias_part), ('dp', 'tile'))  348 us
    ppermute x2, waiting for transfers between devices, with_halo(): lax.ppermute(tail, axis, [(i, (i + 1) % count) for i in range(ends)])  229 us
    psum x1, blocking collectives, local(): lax.psum((kernel_part, gain_part, bias_part), ('dp', 'tile'))  108 us
    all_to_all x1, starting transfers between devices, bring_signs_by_axis(): jax.lax.all_to_all(jnp.stack(jax.lax.axis_size(group_axis) * [in_array]),...  18.5 us
  transfers between devices with their start and end apart: 7, of which 4 were waited for; matrix products, arithmetic and copies ran while one was open for 4% of the time, Pallas kernels for 0%

profile of v1, /device:TPU:1, one launch (start us, length us, event | category | flops | bytes accessed | tf_op | source)
XLA Modules:
  0.0 786.5 jit_solution(16127299949530987927)
XLA Ops:
  7.2 3.4 stack.259
  10.6 18.5 %all-to-all-start = ((bf16[64,48,768]{2,1,0:T(8,128)(2,1)}), bf16[64,48,768]{2,1,0:T(8,128)(2,1)}, u32[]{:S(2)}, u32[]{:S(2)}) async-start(bf16[64,48,768]{2,1,0:T(8,128)(2,1)} %stack.259), calls=%async_computation | async-start | bytes 9437184 | tf_op jit(solution)/shard_map/all_to_all | solution.py:12
  29.1 0.7 all-gather.3.cloned.1.call-update
  29.9 3.5 collective-permute-start
  33.4 1.9 collective-permute-start.1
  35.4 0.8 broadcast_multiply_fusion
  36.7 228.8 %collective-permute-done = bf16[1,3,64,768]{3,2,1,0:T(8,128)(2,1)S(1)} collective-permute-done((bf16[1,3,64,768]{3,2,1,0:T(8,128)(2,1)S(1)}, bf16[1,3,64,768]{3,2,1,0:T(8,128)(2,1)S(1)}, u32[]{:S(2)}, u32[]{:S(2)}) %collective-permute-start) | collective-permute-done | bytes 294944 | tf_op jit(solution)/shard_map/ppermute | solution.py:29
  265.6 2.9 collective-permute-done.1
  268.6 0.3 fusion.12
  268.9 6.5 fusion.124
  275.4 0.2 multiply_reduce_fusion.3
  275.7 0.9 multiply_convert_fusion.1
  276.6 0.2 all-gather.3.cloned.1.call-done
  276.8 7.6 reshape.400
  284.3 5.5 convolution_add_fusion
  289.9 7.3 convert_reduce_fusion
  297.2 1.5 multiply_reduce_fusion.2
  298.7 0.9 copy-done.3
  299.6 0.9 multiply_reduce_fusion
  300.4 0.6 broadcast_multiply_fusion.1
  301.0 0.7 div.17
  301.7 4.0 fusion.118
  305.7 1.2 fusion.117
  306.9 2.0 fusion.119
  309.6 2.4 collective-permute-start.2
  312.1 2.1 collective-permute-start.3
  314.7 0.7 copy-done.8
  315.4 107.7 %all-reduce.2 = (f32[768]{0:T(1024)}, f32[3072]{0:T(1024)}) all-reduce(f32[768]{0:T(1024)S(1)} %copy-done.25, f32[3072]{0:T(1024)S(1)} %copy-done.26), channel_id=1, replica_groups=mesh['dp'=8,'tile'=64] {'dp','tile'}, use_global_device_ids=true, to_apply=%region_55.56 | all-reduce | flops 3840 | bytes 30720 | tf_op jit(solution)/shard_map/psum | solution.py:128
  423.1 0.3 select_maximum_fusion
  423.5 6.5 fusion.70
  430.0 348.1 %all-reduce.5.cloned.1.call-done = f32[7,7,768]{2,1,0:T(8,128)} async-done(((f32[7,7,768]{2,1,0:T(8,128)}), f32[7,7,768]{2,1,0:T(8,128)}) %all-reduce.5.cloned.1.call-update) | async-done | bytes 150544 | tf_op jit(solution)/shard_map/psum | solution.py:128
  778.1 1.6 copy.21
  (135 shorter events, 1.4 us)
Async XLA Ops:
  10.6 19.3 %copy-start = (bf16[1,4,64,768]{3,2,1,0:T(8,128)(2,1)S(1)}, bf16[1,4,64,768]{3,2,1,0:T(8,128)(2,1)}, u32[]{:S(2)}) copy-start(bf16[1,4,64,768]{3,2,1,0:T(8,128)(2,1)} %param.8) | copy-start | bytes 1179652
  10.6 24.8 %copy-start.27 = (s32[4]{0:T(128)S(1)}, s32[4]{0:T(128)}, u32[]{:S(2)}) copy-start(s32[4]{0:T(128)} %param.15) | copy-start | bytes 52
  10.6 24.8 %copy-start.5 = (bf16[1,4,64,768]{3,2,1,0:T(8,128)(2,1)S(1)}, bf16[1,4,64,768]{3,2,1,0:T(8,128)(2,1)}, u32[]{:S(2)}) copy-start(bf16[1,4,64,768]{3,2,1,0:T(8,128)(2,1)} %param.9) | copy-start | bytes 1179652
  10.6 25.7 %copy-start.9 = (f32[7,7,768]{2,1,0:T(8,128)S(1)}, f32[7,7,768]{2,1,0:T(8,128)}, u32[]{:S(2)}) copy-start(f32[7,7,768]{2,1,0:T(8,128)} %param.10) | copy-start | bytes 451588
  10.6 279.3 %all-to-all-start = ((bf16[64,48,768]{2,1,0:T(8,128)(2,1)}), bf16[64,48,768]{2,1,0:T(8,128)(2,1)}, u32[]{:S(2)}, u32[]{:S(2)}) async-start(bf16[64,48,768]{2,1,0:T(8,128)(2,1)} %stack.259), calls=%async_computation | async-start | bytes 9437184 | tf_op jit(solution)/shard_map/all_to_all | solution.py:12
  29.0 247.7 %all-gather.3.cloned.1.call-start = ((), (), s32[]{:S(2)}) async-start(), calls=%async_computation.2 | async-start | bytes 6389760 | tf_op jit(solution)/shard_map/all_gather | solution.py:85
  29.8 748.3 %all-reduce.5.cloned.1.call-start = ((), (), s32[]{:S(2)}) async-start(), calls=%async_computation.1 | async-start | bytes 344064 | tf_op jit(solution)/shard_map/psum | solution.py:128
  29.9 235.6 %collective-permute-start = (bf16[1,3,64,768]{3,2,1,0:T(8,128)(2,1)S(1)}, bf16[1,3,64,768]{3,2,1,0:T(8,128)(2,1)S(1)}, u32[]{:S(2)}, u32[]{:S(2)}) collective-permute-start(bf16[1,3,64,768]{3,2,1,0:T(8,128)(2,1)S(1)} %get-tuple-element.119), channel_id=1, source_target_pairs={{0,1},{1,2},{2,3},{3,4},{4,5},{5,6},{6,7},{7,8},{8,9},{9,10},{10,1... | collective-permute-start | bytes 884744 | tf_op jit(solution)/shard_map/ppermute | solution.py:29
  33.4 235.1 %collective-permute-start.1 = (bf16[1,3,64,768]{3,2,1,0:T(8,128)(2,1)S(1)}, bf16[1,3,64,768]{3,2,1,0:T(8,128)(2,1)S(1)}, u32[]{:S(2)}, u32[]{:S(2)}) collective-permute-start(bf16[1,3,64,768]{3,2,1,0:T(8,128)(2,1)S(1)} %get-tuple-element.120), channel_id=1, source_target_pairs={{1,0},{2,1},{3,2},{4,3},{5,4},{6,5},{7,6},{8,7},{9,8},{10,9},{11,1... | collective-permute-start | bytes 884744 | tf_op jit(solution)/shard_map/ppermute | solution.py:31
  36.7 232.2 %copy-start.11 = (f32[768]{0:T(1024)}, f32[768]{0:T(1024)S(1)}, u32[]{:S(2)}) copy-start(f32[768]{0:T(1024)S(1)} %get-tuple-element.105) | copy-start | bytes 9220
  36.7 232.2 %copy-start.13 = (f32[768]{0:T(1024)}, f32[768]{0:T(1024)S(1)}, u32[]{:S(2)}) copy-start(f32[768]{0:T(1024)S(1)} %get-tuple-element.106) | copy-start | bytes 9220
  36.7 232.2 %copy-start.15 = (f32[768]{0:T(1024)}, f32[768]{0:T(1024)S(1)}, u32[]{:S(2)}) copy-start(f32[768]{0:T(1024)S(1)} %get-tuple-element.107) | copy-start | bytes 9220
  36.7 232.2 %copy-start.17 = (f32[768]{0:T(1024)}, f32[768]{0:T(1024)S(1)}, u32[]{:S(2)}) copy-start(f32[768]{0:T(1024)S(1)} %get-tuple-element.108) | copy-start | bytes 9220
  36.7 232.2 %copy-start.19 = (f32[768]{0:T(1024)}, f32[768]{0:T(1024)S(1)}, u32[]{:S(2)}) copy-start(f32[768]{0:T(1024)S(1)} %get-tuple-element.109) | copy-start | bytes 9220
  265.6 9.8 %copy-start.1 = (bf16[1,7,64,768]{3,2,1,0:T(8,128)(2,1)}, bf16[1,7,64,768]{3,2,1,0:T(8,128)(2,1)S(1)}, u32[]{:S(2)}) copy-start(bf16[1,7,64,768]{3,2,1,0:T(8,128)(2,1)S(1)} %get-tuple-element.117) | copy-start | bytes 2064388
  268.9 6.7 copy-start.10
  275.7 8.7 %copy-start.21 = (f32[4,64]{1,0:T(4,128)}, f32[4,64]{1,0:T(4,128)S(1)}, u32[]{:S(2)}) copy-start(f32[4,64]{1,0:T(4,128)S(1)} %add_rsqrt_fusion) | copy-start | bytes 3076
  284.3 5.5 copy-start.7
  289.9 7.3 copy-start.4
  301.7 4.0 copy-start.2
  306.9 7.7 copy-start.24
  306.9 7.7 copy-start.23
  308.9 6.4 copy-start.25
  309.0 6.4 copy-start.26
  309.0 114.4 %copy-start.6 = (bf16[1,4,64,768]{3,2,1,0:T(8,128)(2,1)S(1)}, bf16[1,4,64,768]{3,2,1,0:T(8,128)(2,1)}, u32[]{:S(2)}) copy-start(bf16[1,4,64,768]{3,2,1,0:T(8,128)(2,1)} %param.9) | copy-start | bytes 1179652
  309.0 114.4 %copy-start.12 = (f32[768]{0:T(1024)S(1)}, f32[768]{0:T(1024)}, u32[]{:S(2)}) copy-start(f32[768]{0:T(1024)} %copy-done.11) | copy-start | bytes 9220
  309.0 114.4 %copy-start.14 = (f32[768]{0:T(1024)S(1)}, f32[768]{0:T(1024)}, u32[]{:S(2)}) copy-start(f32[768]{0:T(1024)} %copy-done.13) | copy-start | bytes 9220
  309.0 114.4 %copy-start.16 = (f32[768]{0:T(1024)S(1)}, f32[768]{0:T(1024)}, u32[]{:S(2)}) copy-start(f32[768]{0:T(1024)} %copy-done.15) | copy-start | bytes 9220
  309.0 114.4 %copy-start.18 = (f32[768]{0:T(1024)S(1)}, f32[768]{0:T(1024)}, u32[]{:S(2)}) copy-start(f32[768]{0:T(1024)} %copy-done.17) | copy-start | bytes 9220
  309.0 114.4 %copy-start.20 = (f32[768]{0:T(1024)S(1)}, f32[768]{0:T(1024)}, u32[]{:S(2)}) copy-start(f32[768]{0:T(1024)} %copy-done.19) | copy-start | bytes 9220
  309.6 113.4 %collective-permute-start.2 = (bf16[1,3,64,768]{3,2,1,0:T(8,128)(2,1)S(1)}, bf16[1,3,64,768]{3,2,1,0:T(8,128)(2,1)S(1)}, u32[]{:S(2)}, u32[]{:S(2)}) collective-permute-start(bf16[1,3,64,768]{3,2,1,0:T(8,128)(2,1)S(1)} %get-tuple-element.115), channel_id=1, source_target_pairs={{0,1},{1,2},{2,3},{3,4},{4,5},{5,6},{6,7},{7,8},{8,9},{9,10},{10,1... | collective-permute-start | bytes 884744 | tf_op jit(solution)/shard_map/ppermute | solution.py:29
  312.1 111.0 %collective-permute-start.3 = (bf16[1,3,64,768]{3,2,1,0:T(8,128)(2,1)S(1)}, bf16[1,3,64,768]{3,2,1,0:T(8,128)(2,1)S(1)}, u32[]{:S(2)}, u32[]{:S(2)}) collective-permute-start(bf16[1,3,64,768]{3,2,1,0:T(8,128)(2,1)S(1)} %get-tuple-element.116), channel_id=1, source_target_pairs={{1,0},{2,1},{3,2},{4,3},{5,4},{6,5},{7,6},{8,7},{9,8},{10,9},{11,1... | collective-permute-start | bytes 884744 | tf_op jit(solution)/shard_map/ppermute | solution.py:31
  (3 other events, 3.9 us)
Sparse Core Ops, SparseCore 0:
  32.0 244.7 all-gather.2
  315.5 462.5 all-reduce.4
